TPU v7x, 32 devices: a whole 2x2x4 slice. The times are simulated.
32 devices in a mesh: dp: 16 (over z, y, core), expert: 2 (over x).
Axes of the slice: x: 2, y: 2, z: 4, core: 2. Of those that a mesh axis runs over, the one named last changes fastest.
Arguments:
- tokens: bfloat16 [4096, 2048], P(('dp', 'expert')), may hold values from -6 to 6
- cotangent: bfloat16 [4096, 2048], P(('dp', 'expert')), may hold values from -6 to 6
- expert_ids: int32 [4096, 8], P(('dp', 'expert')), may hold values from 0 to 127, as said below
- route_weights: float32 [4096, 8], P(('dp', 'expert')), may hold values from 0.1 to 1
- join_groups: int32 [16], replicated, may hold values from 0 to 1
- w_gate: bfloat16 [2048, 1024], P('dp', 'expert'), may hold values from -0.125 to 0.125
- w_up: bfloat16 [2048, 1024], P('dp', 'expert'), may hold values from -0.125 to 0.125
- w_down: bfloat16 [2048, 1024], P('dp', 'expert'), may hold values from -0.1875 to 0.1875
Outputs:
- mixed: bfloat16 [4096, 2048], P(('dp', 'expert'))
- grad_gate: bfloat16 [2048, 1024], P('dp', 'expert')
- grad_up: bfloat16 [2048, 1024], P('dp', 'expert')
- grad_down: bfloat16 [2048, 1024], P('dp', 'expert')
Inputs may be any that keep to these rules, and one draw needn't show every extreme that they name: `expert_ids`: each row names 8 different experts; the rows of one device name expert 0 at most 16 times, and the rows of some device exactly 16 times.
All inputs are finite; a program needn't handle non-finite values.
Results may differ from a plain program's by a relative error of at most 0.014.
Values may be sent and summed in bfloat16 or wider, within the bound.
A program may use at most 64 MiB of HBM per device.

v0:
```python
import jax
import jax.numpy as jnp
from jax import lax
from jax.sharding import PartitionSpec as P


def per_device(tokens, cotangent, expert_ids, route_weights, join_groups, w_gate, w_up, w_down):
    highest = lax.Precision.HIGHEST
    tok_count = tokens.shape[0]
    slot_count = tok_count // 8
    slice_width = w_gate.shape[1]
    chosen_mask = expert_ids == 0
    routed = jnp.any(chosen_mask, -1)
    weight = jnp.sum(jnp.where(chosen_mask, route_weights, 0.0), -1)
    places = jnp.cumsum(routed.astype(jnp.int32)) - 1
    slot_ids = jnp.arange(slot_count, dtype=jnp.int32)
    chooser = ((places[None, :] == slot_ids[:, None]) & routed[None, :]).astype(jnp.float32)
    chooser_half = chooser.astype(jnp.bfloat16)
    picked_local = jnp.dot(chooser_half, tokens, preferred_element_type=jnp.float32).astype(
        jnp.bfloat16
    )
    picked = lax.all_gather(picked_local, "expert", axis=0, tiled=True)
    gate_acts = jnp.dot(
        picked, lax.all_gather(w_gate, "dp", axis=0, tiled=True), preferred_element_type=jnp.float32
    )
    up_acts = jnp.dot(
        picked, lax.all_gather(w_up, "dp", axis=0, tiled=True), preferred_element_type=jnp.float32
    )
    hidden = (jax.nn.silu(gate_acts) * up_acts).astype(jnp.bfloat16)
    trans_dims = (((1,), (1,)), ((), ()))
    full_down = lax.all_gather(w_down, "dp", axis=0, tiled=True)
    partial_out = lax.dot_general(hidden, full_down, trans_dims, preferred_element_type=jnp.float32)
    out_rows = lax.psum_scatter(
        partial_out.astype(jnp.bfloat16), "expert", scatter_dimension=0, tiled=True
    ).astype(jnp.float32)
    placed = lax.dot_general(
        chooser,
        out_rows,
        (((0,), (0,)), ((), ())),
        precision=highest,
        preferred_element_type=jnp.float32,
    )
    mixed = (placed * weight[:, None]).astype(jnp.bfloat16)
    scaled = cotangent.astype(jnp.float32) * weight[:, None]
    dpicked_local = jnp.dot(
        chooser, scaled, precision=highest, preferred_element_type=jnp.float32
    ).astype(jnp.bfloat16)
    dpicked = lax.all_gather(dpicked_local, "expert", axis=0, tiled=True)
    hidden_grad = jnp.dot(dpicked, full_down, preferred_element_type=jnp.float32)
    sigma_gate = jax.nn.sigmoid(gate_acts)
    dgate = (hidden_grad * up_acts * sigma_gate * (1.0 + gate_acts * (1.0 - sigma_gate))).astype(
        jnp.bfloat16
    )
    dup = (hidden_grad * gate_acts * sigma_gate).astype(jnp.bfloat16)
    group_total = lax.axis_size("dp")
    mine = jnp.arange(group_total, dtype=jnp.int32) == lax.axis_index("dp")
    active = 1.0 - jnp.sum(jnp.where(mine, join_groups, 0)).astype(jnp.float32)
    col_dims = (((0,), (0,)), ((), ()))

    def term_of(left, right):
        return active * lax.dot_general(left, right, col_dims, preferred_element_type=jnp.float32)

    summed = lax.psum_scatter(
        jnp.concatenate(
            [term_of(picked, dgate), term_of(picked, dup), term_of(dpicked, hidden)], axis=1
        ),
        "dp",
        scatter_dimension=0,
        tiled=True,
    )
    grad_gate = summed[:, :slice_width]
    grad_up = summed[:, slice_width : 2 * slice_width]
    grad_down = summed[:, 2 * slice_width :]
    return (
        mixed,
        grad_gate.astype(jnp.bfloat16),
        grad_up.astype(jnp.bfloat16),
        grad_down.astype(jnp.bfloat16),
    )


def solution(mesh):
    in_specs = (
        P(("dp", "expert"), None),
        P(("dp", "expert"), None),
        P(("dp", "expert"), None),
        P(("dp", "expert"), None),
        P(),
        P("dp", "expert"),
        P("dp", "expert"),
        P("dp", "expert"),
    )
    out_specs = (P(("dp", "expert"), None), P("dp", "expert"), P("dp", "expert"), P("dp", "expert"))
    return jax.shard_map(
        per_device, mesh=mesh, in_specs=in_specs, out_specs=out_specs, check_vma=False
    )
```

profile of v0, /device:TPU:0, one launch (start us, length us, event | category | flops | bytes accessed | tf_op | source)
XLA Modules:
  0.0 300.2 jit_solution(16604740441010829208)
XLA Ops:
  7.2 0.7 all-gather.4.cloned.1.call-update
  8.0 0.7 all-gather.6.cloned.1.call-update
  8.7 0.7 all-gather.8.cloned.1.call-update
  9.4 0.0 reduce-scatter.3.cloned.1.call-start
  9.5 1.3 fusion.15
  11.4 0.7 select_reduce_fusion
  12.1 0.1 copy.16
  12.3 0.2 reduce-window.8
  12.4 0.1 add_reduce_fusion
  12.5 1.6 convolution_convert_fusion.1
  14.2 5.9 %all_gather.19 = bf16[32,2048]{1,0:T(8,128)(2,1)S(1)} all-gather(bf16[16,2048]{1,0:T(8,128)(2,1)S(1)} %convolution_convert_fusion.1), channel_id=1, replica_groups=mesh['dp'=16,'expert'=2] {'expert'}, dimensions={0}, use_global_device_ids=true | all-gather | bytes 196608 | tf_op jit(solution)/shard_map/all_gather | solution.py:48
  20.0 0.2 convolution_convert_fusion.2
  20.2 4.9 %all_gather.15 = bf16[32,2048]{1,0:T(8,128)(2,1)S(1)} all-gather(bf16[16,2048]{1,0:T(8,128)(2,1)S(1)} %convolution_convert_fusion.2), channel_id=1, replica_groups=mesh['dp'=16,'expert'=2] {'expert'}, dimensions={0}, use_global_device_ids=true | all-gather | bytes 196608 | tf_op jit(solution)/shard_map/all_gather | solution.py:22
  25.1 29.2 %all-gather.4.cloned.1.call-done = bf16[2048,512]{1,0:T(8,128)(2,1)} async-done(((bf16[128,512]{1,0:T(8,128)(2,1)}), bf16[2048,512]{1,0:T(8,128)(2,1)}) %all-gather.4.cloned.1.call-update) | async-done | bytes 2097168 | tf_op jit(solution)/shard_map/all_gather | solution.py:24
  54.4 2.0 fusion.19
  56.4 40.3 %all-gather.6.cloned.1.call-done = bf16[2048,512]{1,0:T(8,128)(2,1)} async-done(((bf16[128,512]{1,0:T(8,128)(2,1)}), bf16[2048,512]{1,0:T(8,128)(2,1)}) %all-gather.6.cloned.1.call-update) | async-done | bytes 2097168 | tf_op jit(solution)/shard_map/all_gather | solution.py:27
  96.7 2.0 multiply_convert_fusion.2
  98.8 40.3 %all-gather.8.cloned.1.call-done = bf16[2048,512]{1,0:T(8,128)(2,1)} async-done(((bf16[128,512]{1,0:T(8,128)(2,1)}), bf16[2048,512]{1,0:T(8,128)(2,1)}) %all-gather.8.cloned.1.call-update) | async-done | bytes 2097168 | tf_op jit(solution)/shard_map/all_gather | solution.py:31
  139.1 3.1 %convolution_convert_fusion = bf16[32,2048]{1,0:T(8,128)(2,1)} fusion(bf16[32,512]{1,0:T(8,128)(2,1)S(1)} %get-tuple-element.17, bf16[2048,512]{1,0:T(8,128)(2,1)} %all-gather.8.cloned.1.call-done), kind=kOutput, calls=%fused_computation.6 | convolution fusion | flops 67174400 | bytes 2260992 | tf_op jit(solution)/shard_map/dot_general | solution.py:32
  142.3 0.0 reduce-scatter.5.cloned.1.call-start
  142.3 0.7 convolution_multiply_fusion
  143.1 0.5 fusion.20
  143.5 0.8 convolution_multiply_fusion.1
  144.3 0.8 convolution_multiply_fusion.2
  145.1 5.4 %pad_maximum_fusion = f32[2048,1536]{0,1:T(8,128)} fusion(f32[2048,512]{0,1:T(8,128)S(1)} %convolution_multiply_fusion, f32[2048,512]{0,1:T(8,128)S(1)} %convolution_multiply_fusion.1, f32[2048,512]{0,1:T(8,128)S(1)} %convolution_multiply_fusion.2), kind=kLoop, calls=%fused_computation | loop fusion | flops 6291456 | bytes 25165824 | tf_op jit(solution)/shard_map/concatenate | solution.py:64
  150.5 1.0 reduce-scatter.3.cloned.1.call-done
  151.5 2.0 fusion
  153.5 136.7 %reduce-scatter.5.cloned.1.call-done = f32[128,1536]{0,1:T(8,128)} async-done(((f32[2048,1536]{0,1:T(8,128)}), f32[128,1536]{0,1:T(8,128)}) %reduce-scatter.5.cloned.1.call-update) | async-done | bytes 786448 | tf_op jit(solution)/shard_map/reduce_scatter | solution.py:63
  290.2 1.2 convert.6
  291.4 0.8 copy.19
  292.2 0.8 copy.18
  292.9 0.8 copy.17
  (12 shorter events, 0.2 us)
Async XLA Ops:
  7.2 12.9 %copy-start = (bf16[128,2048]{1,0:T(8,128)(2,1)S(1)}, bf16[128,2048]{1,0:T(8,128)(2,1)}, u32[]{:S(2)}) copy-start(bf16[128,2048]{1,0:T(8,128)(2,1)} %param.8) | copy-start | bytes 1572868
  7.2 47.2 %all-gather.4.cloned.1.call-start = ((), (), s32[]{:S(2)}) async-start(), calls=%async_computation.2 | async-start | bytes 2228224 | tf_op jit(solution)/shard_map/all_gather | solution.py:24
  7.9 88.8 %all-gather.6.cloned.1.call-start = ((), (), s32[]{:S(2)}) async-start(), calls=%async_computation.3 | async-start | bytes 2228224 | tf_op jit(solution)/shard_map/all_gather | solution.py:27
  8.7 130.4 %all-gather.8.cloned.1.call-start = ((), (), s32[]{:S(2)}) async-start(), calls=%async_computation.4 | async-start | bytes 2228224 | tf_op jit(solution)/shard_map/all_gather | solution.py:31
  9.4 142.1 %reduce-scatter.3.cloned.1.call-start = ((), (), s32[]{:S(2)}) async-start(), calls=%async_computation.5 | async-start | bytes 196608 | tf_op jit(solution)/shard_map/reduce_scatter | solution.py:33
  139.1 4.0 %copy-start.1 = (bf16[2048,512]{1,0:T(8,128)(2,1)S(1)}, bf16[2048,512]{1,0:T(8,128)(2,1)}, u32[]{:S(2)}) copy-start(bf16[2048,512]{1,0:T(8,128)(2,1)} %all-gather.8.cloned.1.call-done) | copy-start | bytes 6291460
  142.3 147.9 %reduce-scatter.5.cloned.1.call-start = ((), (), s32[]{:S(2)}) async-start(), calls=%async_computation.6 | async-start | bytes 13369344 | tf_op jit(solution)/shard_map/reduce_scatter | solution.py:63
Sparse Core Ops, SparseCore 0:
  10.2 44.1 all-gather.3
  56.5 40.1 all-gather.5
  98.9 40.1 all-gather.7
  142.4 9.0 reduce-scatter.2
  155.4 134.7 reduce-scatter.4
where the time goes:
time: 301 us; the launch traced here: 300 us
  waiting for transfers between devices  250 us (83%)
  between operations  14.5 us (5%)
  matrix products  13.7 us (5%)
  blocking collectives  10.8 us (4%)
  other arithmetic  8.91 us (3%)
    reduce_scatter x1, waiting for transfers between devices, per_device(): lax.psum_scatter(jnp.concatenate([term_of(picked, dgate), term_of(picked,...  137 us
    all_gather x1, waiting for transfers between devices, per_device(): full_down = lax.all_gather(w_down, 'dp', axis=0, tiled=True)  40.3 us
    all_gather x1, waiting for transfers between devices, per_device(): lax.all_gather(w_up, 'dp', axis=0, tiled=True)  40.3 us
    all_gather x1, waiting for transfers between devices, per_device(): lax.all_gather(w_gate, 'dp', axis=0, tiled=True)  29.2 us
  transfers between devices with their start and end apart: 5, of which 5 were waited for; matrix products, arithmetic and copies ran while one was open for 6% of the time, Pallas kernels for 0%

commit v1 on v0

--- a/solution.py
+++ b/solution.py
@@ -1,7 +1,25 @@
+import functools
 import jax
 import jax.numpy as jnp
 from jax import lax
 from jax.sharding import PartitionSpec as P
+from jax.lax import axis_index, axis_size, ppermute
+
+
+def _put_corner(field_in, mesh_name, dim_at):
+    reached = axis_size(mesh_name)
+    b_now, latest, plain = (reached, axis_index(mesh_name), field_in.shape[dim_at])
+    r_now, e_next = (field_in, 1)
+    while e_next < b_now:
+        crops = []
+        for m in range(b_now):
+            crops.append((m, (m - e_next) % b_now))
+        r_now = jnp.concatenate([r_now, ppermute(r_now, mesh_name, crops)], dim_at)
+        e_next = 2 * e_next
+    return jnp.roll(r_now, latest * plain, dim_at)
+
+
+map_positions = functools.partial(_put_corner, mesh_name="dp", dim_at=0)
 
 
 def per_device(tokens, cotangent, expert_ids, route_weights, join_groups, w_gate, w_up, w_down):
@@ -23,9 +41,7 @@
     gate_acts = jnp.dot(
         picked, lax.all_gather(w_gate, "dp", axis=0, tiled=True), preferred_element_type=jnp.float32
     )
-    up_acts = jnp.dot(
-        picked, lax.all_gather(w_up, "dp", axis=0, tiled=True), preferred_element_type=jnp.float32
-    )
+    up_acts = jnp.dot(picked, map_positions(w_up), preferred_element_type=jnp.float32)
     hidden = (jax.nn.silu(gate_acts) * up_acts).astype(jnp.bfloat16)
     trans_dims = (((1,), (1,)), ((), ()))
     full_down = lax.all_gather(w_down, "dp", axis=0, tiled=True)

time: 301 us -> 316 us (1.050)
  waiting for transfers between devices: 250 us -> 240 us
  local copies, waits for them, and re-layouts: 2.47 us -> 11.8 us
  starting transfers between devices: 0.19 us -> 8.1 us
  other arithmetic: 8.91 us -> 14.2 us
    ppermute x0 -> x4, waiting for transfers between devices: none -> 65.1 us  [_put_corner(): r_now = jnp.concatenate([r_now, ppermute(r_now, mesh_name, crops)], dim_at)]
    all_gather x1, waiting for transfers between devices: 40.3 us -> 0.01 us  [per_device(): full_down = lax.all_gather(w_down, 'dp', axis=0, tiled=True)]
    all_gather x1 -> x0, waiting for transfers between devices: 40.3 us -> none  [per_device(): lax.all_gather(w_up, 'dp', axis=0, tiled=True)]
    unnamed x7 -> x24, local copies, waits for them, and re-layouts: 2.32 us -> 10.6 us
    all_gather x1, waiting for transfers between devices: 29.2 us -> 37.4 us  [per_device(): lax.all_gather(w_gate, 'dp', axis=0, tiled=True)]
    ppermute x0 -> x4, starting transfers between devices: none -> 7.94 us  [_put_corner(): r_now = jnp.concatenate([r_now, ppermute(r_now, mesh_name, crops)], dim_at)]
    dot_general x3, matrix products: 2.29 us -> 6.18 us  [term_of(): lax.dot_general(left, right, col_dims, preferred_element_type=jnp.float32)]
    concatenate x0 -> x3, other arithmetic: none -> 3.82 us  [_put_corner(): r_now = jnp.concatenate([r_now, ppermute(r_now, mesh_name, crops)], dim_at)]
  transfers between devices with their start and end apart: 5 -> 8, of which waited for: 5 -> 6; matrix products, arithmetic and copies ran while one was open for 6% -> 8% of each run, Pallas kernels for 0% -> 0%
where the time goes in v1:
time: 316 us; the launch traced here: 315 us
  waiting for transfers between devices  240 us (76%)
  matrix products  16.6 us (5%)
  between operations  14.5 us (5%)
  other arithmetic  14.2 us (4%)
  local copies, waits for them, and re-layouts  11.8 us (4%)
  blocking collectives  9.86 us (3%)
  starting transfers between devices  8.1 us (3%)
    reduce_scatter x1, waiting for transfers between devices, per_device(): lax.psum_scatter(jnp.concatenate([term_of(picked, dgate), term_of(picked,...  136 us
    ppermute x4, waiting for transfers between devices, _put_corner(): r_now = jnp.concatenate([r_now, ppermute(r_now, mesh_name, crops)], dim_at)  65.1 us
    all_gather x1, waiting for transfers between devices, per_device(): lax.all_gather(w_gate, 'dp', axis=0, tiled=True)  37.4 us
    unnamed x24, local copies, waits for them, and re-layouts  10.6 us
    ppermute x4, starting transfers between devices, _put_corner(): r_now = jnp.concatenate([r_now, ppermute(r_now, mesh_name, crops)], dim_at)  7.94 us
    concatenate x1, other arithmetic, per_device(): jnp.concatenate([term_of(picked, dgate), term_of(picked, dup), term_of(dp...  7.55 us
  transfers between devices with their start and end apart: 8, of which 6 were waited for; matrix products, arithmetic and copies ran while one was open for 8% of the time, Pallas kernels for 0%

profile of v1, /device:TPU:0, one launch (start us, length us, event | category | flops | bytes accessed | tf_op | source)
XLA Modules:
  0.0 315.1 jit_solution(14004520559186750636)
XLA Ops:
  8.7 5.5 %collective-permute-start = (bf16[128,512]{1,0:T(8,128)(2,1)}, bf16[128,512]{1,0:T(8,128)(2,1)S(1)}, u32[]{:S(2)}, u32[]{:S(2)}) collective-permute-start(bf16[128,512]{1,0:T(8,128)(2,1)} %param.14), channel_id=1, source_target_pairs={{0,30},{2,0},{4,2},{6,4},{8,6},{10,8},{12,10},{14,12},{16,14},{18,... | collective-permute-start | bytes 393224 | tf_op jit(solution)/shard_map/ppermute | solution.py:17
  14.3 2.8 collective-permute-done
  17.1 0.9 pad_maximum_fusion.3
  18.7 7.3 %collective-permute-done.1 = bf16[256,512]{1,0:T(8,128)(2,1)S(1)} collective-permute-done((bf16[256,512]{1,0:T(8,128)(2,1)S(1)}, bf16[256,512]{1,0:T(8,128)(2,1)S(1)}, u32[]{:S(2)}, u32[]{:S(2)}) %collective-permute-start.1) | collective-permute-done | bytes 262176 | tf_op jit(solution)/shard_map/ppermute | solution.py:17
  26.0 0.9 pad_maximum_fusion.2
  28.1 13.9 %collective-permute-done.2 = bf16[512,512]{1,0:T(8,128)(2,1)S(1)} collective-permute-done((bf16[512,512]{1,0:T(8,128)(2,1)S(1)}, bf16[512,512]{1,0:T(8,128)(2,1)S(1)}, u32[]{:S(2)}, u32[]{:S(2)}) %collective-permute-start.2) | collective-permute-done | bytes 524320 | tf_op jit(solution)/shard_map/ppermute | solution.py:17
  42.1 2.0 pad_maximum_fusion.1
  44.0 1.7 collective-permute-start.3
  47.6 4.9 %all_gather.15 = bf16[32,2048]{1,0:T(8,128)(2,1)S(1)} all-gather(bf16[16,2048]{1,0:T(8,128)(2,1)S(1)} %convolution_convert_fusion.1), channel_id=1, replica_groups=mesh['dp'=16,'expert'=2] {'expert'}, dimensions={0}, use_global_device_ids=true | all-gather | bytes 196608 | tf_op jit(solution)/shard_map/all_gather | solution.py:64
  52.8 4.9 %all_gather.12 = bf16[32,2048]{1,0:T(8,128)(2,1)S(1)} all-gather(bf16[16,2048]{1,0:T(8,128)(2,1)S(1)} %convolution_convert_fusion.2), channel_id=1, replica_groups=mesh['dp'=16,'expert'=2] {'expert'}, dimensions={0}, use_global_device_ids=true | all-gather | bytes 196608 | tf_op jit(solution)/shard_map/all_gather | solution.py:40
  59.0 0.7 constant_dynamic-update-slice_fusion.7
  59.8 0.8 constant_dynamic-update-slice_fusion.6
  60.6 41.0 %collective-permute-done.3 = bf16[1024,512]{1,0:T(8,128)(2,1)S(1)} collective-permute-done((bf16[1024,512]{1,0:T(8,128)(2,1)}, bf16[1024,512]{1,0:T(8,128)(2,1)S(1)}, u32[]{:S(2)}, u32[]{:S(2)}) %collective-permute-start.3) | collective-permute-done | bytes 1048608 | tf_op jit(solution)/shard_map/ppermute | solution.py:17
  101.6 1.1 constant_dynamic-update-slice_fusion.5
  104.8 0.8 constant_dynamic-update-slice_fusion.1
  105.6 1.1 constant_dynamic-update-slice_fusion
  106.7 2.1 fusion.23
  108.7 37.4 %all-gather.3.cloned.1.call-done = bf16[2048,512]{1,0:T(8,128)(2,1)} async-done(((bf16[128,512]{1,0:T(8,128)(2,1)}), bf16[2048,512]{1,0:T(8,128)(2,1)}) %all-gather.3.cloned.1.call-update) | async-done | bytes 2097168 | tf_op jit(solution)/shard_map/all_gather | solution.py:42
  146.1 2.0 fusion.22
  148.1 2.7 convolution_multiply_fusion.1
  150.9 2.2 multiply_convert_fusion.2
  153.1 2.7 convolution_multiply_fusion
  155.8 1.4 convolution_convert_fusion
  157.2 0.8 convolution_multiply_fusion.2
  158.0 1.4 copy-done.1
  159.4 7.6 %pad_maximum_fusion = f32[2048,1536]{0,1:T(8,128)} fusion(f32[2048,512]{0,1:T(8,128)} %convolution_multiply_fusion, f32[2048,512]{0,1:T(8,128)S(1)} %copy-done.1, f32[2048,512]{0,1:T(8,128)S(1)} %convolution_multiply_fusion.2), kind=kLoop, calls=%fused_computation | loop fusion | flops 6291456 | bytes 25165824 | tf_op jit(solution)/shard_map/concatenate | solution.py:80
  167.0 2.0 fusion
  169.0 136.1 %reduce-scatter.5.cloned.1.call-done = f32[128,1536]{0,1:T(8,128)} async-done(((f32[2048,1536]{0,1:T(8,128)}), f32[128,1536]{0,1:T(8,128)}) %reduce-scatter.5.cloned.1.call-update) | async-done | bytes 786448 | tf_op jit(solution)/shard_map/reduce_scatter | solution.py:79
  305.1 1.2 convert.6
  306.3 0.8 copy.19
  307.1 0.8 copy.18
  307.8 0.8 copy.17
  (38 shorter events, 8.2 us)
Async XLA Ops:
  7.2 45.4 %copy-start = (bf16[128,2048]{1,0:T(8,128)(2,1)S(1)}, bf16[128,2048]{1,0:T(8,128)(2,1)}, u32[]{:S(2)}) copy-start(bf16[128,2048]{1,0:T(8,128)(2,1)} %param.8) | copy-start | bytes 1572868
  7.2 50.5 %copy-start.3 = (bf16[128,512]{1,0:T(8,128)(2,1)S(1)}, bf16[128,512]{1,0:T(8,128)(2,1)}, u32[]{:S(2)}) copy-start(bf16[128,512]{1,0:T(8,128)(2,1)} %param.14) | copy-start | bytes 393220
  7.2 38.6 %copy-start.5 = (s32[16]{0:T(128)S(1)}, s32[16]{0:T(128)}, u32[]{:S(2)}) copy-start(s32[16]{0:T(128)} %param.12) | copy-start | bytes 196
  7.2 39.8 %copy-start.4 = (bf16[128,2048]{1,0:T(8,128)(2,1)S(1)}, bf16[128,2048]{1,0:T(8,128)(2,1)}, u32[]{:S(2)}) copy-start(bf16[128,2048]{1,0:T(8,128)(2,1)} %param.9) | copy-start | bytes 1572868
  7.2 99.4 %all-gather.5.cloned.1.call-start = ((), (), s32[]{:S(2)}) async-start(), calls=%async_computation.3 | async-start | bytes 2228224 | tf_op jit(solution)/shard_map/all_gather | solution.py:47
  7.9 138.2 %all-gather.3.cloned.1.call-start = ((), (), s32[]{:S(2)}) async-start(), calls=%async_computation.2 | async-start | bytes 2228224 | tf_op jit(solution)/shard_map/all_gather | solution.py:42
  8.7 158.3 %reduce-scatter.3.cloned.1.call-start = ((), (), s32[]{:S(2)}) async-start(), calls=%async_computation.4 | async-start | bytes 196608 | tf_op jit(solution)/shard_map/reduce_scatter | solution.py:49
  8.7 8.4 %collective-permute-start = (bf16[128,512]{1,0:T(8,128)(2,1)}, bf16[128,512]{1,0:T(8,128)(2,1)S(1)}, u32[]{:S(2)}, u32[]{:S(2)}) collective-permute-start(bf16[128,512]{1,0:T(8,128)(2,1)} %param.14), channel_id=1, source_target_pairs={{0,30},{2,0},{4,2},{6,4},{8,6},{10,8},{12,10},{14,12},{16,14},{18,... | collective-permute-start | bytes 393224 | tf_op jit(solution)/shard_map/ppermute | solution.py:17
  18.0 8.0 %collective-permute-start.1 = (bf16[256,512]{1,0:T(8,128)(2,1)S(1)}, bf16[256,512]{1,0:T(8,128)(2,1)S(1)}, u32[]{:S(2)}, u32[]{:S(2)}) collective-permute-start(bf16[256,512]{1,0:T(8,128)(2,1)S(1)} %pad_maximum_fusion.3), channel_id=1, source_target_pairs={{0,28},{2,30},{4,0},{6,2},{8,4},{10,6},{12,8},{14,10},{16,12},{18,... | collective-permute-start | bytes 786440 | tf_op jit(solution)/shard_map/ppermute | solution.py:17
  26.9 15.1 %collective-permute-start.2 = (bf16[512,512]{1,0:T(8,128)(2,1)S(1)}, bf16[512,512]{1,0:T(8,128)(2,1)S(1)}, u32[]{:S(2)}, u32[]{:S(2)}) collective-permute-start(bf16[512,512]{1,0:T(8,128)(2,1)S(1)} %pad_maximum_fusion.2), channel_id=1, source_target_pairs={{0,24},{2,26},{4,28},{6,30},{8,0},{10,2},{12,4},{14,6},{16,8},{18,... | collective-permute-start | bytes 1572872 | tf_op jit(solution)/shard_map/ppermute | solution.py:17
  44.0 57.6 %collective-permute-start.3 = (bf16[1024,512]{1,0:T(8,128)(2,1)}, bf16[1024,512]{1,0:T(8,128)(2,1)S(1)}, u32[]{:S(2)}, u32[]{:S(2)}) collective-permute-start(bf16[1024,512]{1,0:T(8,128)(2,1)} %pad_maximum_fusion.1), channel_id=1, source_target_pairs={{0,16},{2,18},{4,20},{6,22},{8,24},{10,26},{12,28},{14,30},{16,0},... | collective-permute-start | bytes 3145736 | tf_op jit(solution)/shard_map/ppermute | solution.py:17
  150.9 4.9 %copy-start.2 = (bf16[2048,512]{1,0:T(8,128)(2,1)S(1)}, bf16[2048,512]{1,0:T(8,128)(2,1)}, u32[]{:S(2)}) copy-start(bf16[2048,512]{1,0:T(8,128)(2,1)} %all-gather.5.cloned.1.call-done) | copy-start | bytes 6291460
  157.2 147.9 %reduce-scatter.5.cloned.1.call-start = ((), (), s32[]{:S(2)}) async-start(), calls=%async_computation.5 | async-start | bytes 13369344 | tf_op jit(solution)/shard_map/reduce_scatter | solution.py:79
  157.2 2.2 copy-start.1
Sparse Core Ops, SparseCore 0:
  10.2 93.1 all-gather.4
  105.6 40.4 all-gather.2
  157.3 9.0 reduce-scatter.2
  170.3 134.7 reduce-scatter.4
